TPU v7x, 32 devices: a whole 2x2x4 slice. The times are simulated.
32 devices in a mesh: view: 2 (over y), row: 2 (over x), col: 8 (over z, core).
Axes of the slice: x: 2, y: 2, z: 4, core: 2. Of those that a mesh axis runs over, the one named last changes fastest.
Arguments:
- inputs: bfloat16 [2, 512, 8192], P('view', 'col', 'row'), may hold values from -28 to 28, as said below
- weight: bfloat16 [8192, 8192], P('row', 'col'), may hold values from -0.0625 to 0.0625
Outputs:
- grad_hidden: bfloat16 [2, 512, 8192], P('view', 'col', 'row')
- grad_weight: float32 [8192, 8192], P('row', 'col')
Inputs may be any that keep to these rules, and one draw needn't show every extreme that they name: `inputs`: feature activations of the two views of a clip; each feature has its own scale.
All inputs are finite; a program needn't handle non-finite values.
Results may differ from a plain program's by a relative error of at most 0.025.
Values may be sent and summed in bfloat16 or wider, within the bound.
No kernel may reach another device: no remote copies, remote signals or barrier semaphores. Data moves between devices by JAX's collectives and lax.ppermute only.
A program may use at most 128 MiB of HBM per device.

v0:
```python
import math
import jax
import jax.numpy as jnp
from jax import lax
from jax.sharding import PartitionSpec as P

off_weight = 0.0051
norm_eps = 1e-05


def from_partner(block, axis, distance):
    count = lax.axis_size(axis)
    route = []
    for low in range(count):
        high = low | 1 << distance
        if high != low and high < count:
            route += [(low, high), (high, low)]
    return lax.ppermute(block, axis, route)


def shards(inputs, weight):
    hidden = lax.all_gather(inputs[0], "col", axis=0, tiled=True)
    batch = hidden.shape[0]
    columns = weight
    pre = lax.psum_scatter(
        lax.dot_general(
            columns, hidden, (((0,), (1,)), ((), ())), preferred_element_type=jnp.float32
        ).astype(jnp.bfloat16),
        "row",
        scatter_dimension=0,
        tiled=True,
    ).astype(jnp.float32)
    centred = pre - jnp.mean(pre, axis=1, keepdims=True)
    rstd = lax.rsqrt(jnp.mean(centred * centred, axis=1, keepdims=True) + norm_eps)
    own = (centred * rstd).astype(jnp.bfloat16)
    partner = from_partner(own, "view", 0)
    own_f = own.astype(jnp.float32)
    partner_f = partner.astype(jnp.float32)
    diag = jnp.sum(own_f * partner_f, axis=1, keepdims=True) / batch
    piece = lax.all_gather(partner, ("row", "col"), axis=0, tiled=True)
    corr = (
        lax.dot_general(own, piece, (((1,), (1,)), ((), ())), preferred_element_type=jnp.float32)
        / batch
    )
    mixed = jnp.dot(corr.astype(jnp.bfloat16), piece, preferred_element_type=jnp.float32)
    scale_diag = 2.0 * (diag - 1.0) - 2.0 * off_weight * diag
    dnorm = 2.0 * off_weight * mixed + scale_diag * partner_f
    inner = jnp.mean(dnorm * own_f, axis=1, keepdims=True)
    dpre = (rstd * (dnorm - jnp.mean(dnorm, axis=1, keepdims=True) - own_f * inner)).astype(
        jnp.bfloat16
    )
    grads = lax.all_gather(dpre, "row", axis=0, tiled=True)
    local_weight = lax.dot_general(
        hidden, grads, (((0,), (1,)), ((), ())), preferred_element_type=jnp.float32
    )
    grad_weight = lax.psum(local_weight.astype(jnp.bfloat16), "view").astype(
        jnp.float32
    ) / math.sqrt(2.0 * batch)
    columns = grads
    grad_hidden = lax.psum_scatter(
        lax.dot_general(
            columns, weight, (((0,), (1,)), ((), ())), preferred_element_type=jnp.float32
        ).astype(jnp.bfloat16),
        "col",
        scatter_dimension=0,
        tiled=True,
    )
    return (grad_hidden[None], grad_weight)


def solution(mesh):
    return jax.shard_map(
        shards,
        mesh=mesh,
        in_specs=(P("view", "col", "row"), P("row", "col")),
        out_specs=(P("view", "col", "row"), P("row", "col")),
        check_vma=False,
    )
```

profile of v0, /device:TPU:0, one launch (start us, length us, event | category | flops | bytes accessed | tf_op | source)
XLA Modules:
  0.0 486.3 jit_solution(11138176716313369393)
XLA Ops:
  7.2 0.0 all-gather.9.cloned.1.call-start
  7.2 0.7 all-gather.9.cloned.1.call-update
  7.9 0.0 reduce-scatter.3.cloned.1.call-start
  7.9 51.2 %all-gather.9.cloned.1.call-done = bf16[1,512,4096]{2,1,0:T(8,128)(2,1)} async-done(((bf16[1,64,4096]{2,1,0:T(8,128)(2,1)}), bf16[1,512,4096]{2,1,0:T(8,128)(2,1)}) %all-gather.9.cloned.1.call-update) | async-done | bytes 4194320 | tf_op jit(solution)/shard_map/all_gather | solution.py:22
  59.2 10.1 %fusion.4 = bf16[1024,512]{1,0:T(8,128)(2,1)} fusion(bf16[4096,1024]{1,0:T(8,128)(2,1)} %param.3, bf16[1,512,4096]{2,1,0:T(8,128)(2,1)} %all-gather.9.cloned.1.call-done), kind=kOutput, calls=%fused_computation.11 | convolution fusion | flops 4295491584 | bytes 13631488 | tf_op jit(solution)/shard_map/dot_general | solution.py:26
  69.3 0.0 reduce-scatter.3.cloned.1.call-update
  69.3 0.0 all-gather.5.cloned.1.call-start
  69.4 19.3 %reduce-scatter.3.cloned.1.call-done = bf16[512,512]{1,0:T(8,128)(2,1)} async-done(((bf16[1024,512]{1,0:T(8,128)(2,1)}), bf16[512,512]{1,0:T(8,128)(2,1)}) %reduce-scatter.3.cloned.1.call-update) | async-done | bytes 524304 | tf_op jit(solution)/shard_map/reduce_scatter | solution.py:25
  88.7 1.2 convert_reduce_fusion
  89.9 1.3 fusion.11
  91.2 1.3 fusion.12
  92.5 1.5 collective-permute-start
  94.0 12.0 %collective-permute-done = bf16[512,512]{1,0:T(8,128)(2,1)S(1)} collective-permute-done((bf16[512,512]{1,0:T(8,128)(2,1)S(1)}, bf16[512,512]{1,0:T(8,128)(2,1)S(1)}, u32[]{:S(2)}, u32[]{:S(2)}) %collective-permute-start) | collective-permute-done | bytes 524320 | tf_op jit(solution)/shard_map/ppermute | solution.py:18
  106.0 0.0 copy-start.1
  106.0 0.8 copy-done.1
  106.8 0.0 all-gather.5.cloned.1.call-update
  106.8 0.0 all-gather.7.cloned.1.call-start
  106.9 1.6 fusion.13
  108.5 0.0 copy-start
  108.6 72.7 %all-gather.5.cloned.1.call-done = bf16[8192,512]{1,0:T(8,128)(2,1)} async-done(((bf16[512,512]{1,0:T(8,128)(2,1)}), bf16[8192,512]{1,0:T(8,128)(2,1)}) %all-gather.5.cloned.1.call-update) | async-done | bytes 8388624 | tf_op jit(solution)/shard_map/all_gather | solution.py:40
  181.3 15.2 %fusion.19 = (f32[512]{0:T(512)S(1)}, f32[512]{0:T(512)S(1)}, f32[512,512]{1,0:T(8,128)S(1)}) fusion(bf16[512,512]{1,0:T(8,128)(2,1)S(1)} %fusion.12, bf16[512,512]{1,0:T(8,128)(2,1)} %copy-done.1, f32[512]{0:T(512)S(1)} %multiply_subtract_fusion, bf16[8192,512]{1,0:T(8,128)(2,1)} %all-gather.5.cloned.1.call-done), kind=kOutput, calls=%fused_computation.32 | convolution fusion | flops 8600420352 | bytes 10491904 | tf_op jit(solution)/shard_map/dot_general | solution.py:45
  196.5 0.0 copy-done
  196.6 1.1 fusion.17
  197.7 0.0 all-gather.7.cloned.1.call-update
  197.7 0.2 all-reduce.2.cloned.1.call-start
  197.9 19.8 %all-gather.7.cloned.1.call-done = bf16[1024,512]{1,0:T(8,128)(2,1)} async-done(((bf16[512,512]{1,0:T(8,128)(2,1)}), bf16[1024,512]{1,0:T(8,128)(2,1)}) %all-gather.7.cloned.1.call-update) | async-done | bytes 1048592 | tf_op jit(solution)/shard_map/all_gather | solution.py:52
  217.7 10.4 %convert_bitcast_fusion = bf16[4096,1024]{0,1:T(8,128)(2,1)} fusion(bf16[1024,512]{1,0:T(8,128)(2,1)} %all-gather.7.cloned.1.call-done, bf16[1,512,4096]{2,1,0:T(8,128)(2,1)} %all-gather.9.cloned.1.call-done), kind=kOutput, calls=%fused_computation.2 | convolution fusion | flops 4299161600 | bytes 13631488 | tf_op jit(solution)/shard_map/dot_general | solution.py:53
  228.2 0.0 copy-start.2
  228.2 0.0 all-reduce.2.cloned.1.call-update
  228.2 0.0 reduce-scatter.5.cloned.1.call-start
  228.2 1.1 copy-done.2
  229.4 9.6 %convolution_convert_fusion = bf16[512,4096]{1,0:T(8,128)(2,1)} fusion(bf16[1024,512]{1,0:T(8,128)(2,1)S(1)} %copy-done.2, bf16[4096,1024]{1,0:T(8,128)(2,1)} %param.3), kind=kOutput, calls=%fused_computation.3 | convolution fusion | flops 4297064448 | bytes 13631488 | tf_op jit(solution)/shard_map/dot_general | solution.py:61
  239.0 0.0 reduce-scatter.5.cloned.1.call-update
  239.0 187.4 %all-reduce.2.cloned.1.call-done = bf16[4096,1024]{0,1:T(8,128)(2,1)} async-done(((bf16[4096,1024]{0,1:T(8,128)(2,1)}), bf16[4096,1024]{0,1:T(8,128)(2,1)}) %all-reduce.2.cloned.1.call-update) | async-done | bytes 8388624 | tf_op jit(solution)/shard_map/psum | solution.py:56
  426.4 11.7 %convert_multiply_fusion = f32[4096,1024]{0,1:T(8,128)} fusion(bf16[4096,1024]{0,1:T(8,128)(2,1)} %all-reduce.2.cloned.1.call-done), kind=kLoop, calls=%fused_computation | loop fusion | flops 8388608 | bytes 25165824 | tf_op jit(solution)/shard_map/div | solution.py:56
  438.1 17.5 %copy.5 = f32[4096,1024]{1,0:T(8,128)} copy(f32[4096,1024]{0,1:T(8,128)} %convert_multiply_fusion) | data formatting | bytes 33554432
  455.6 23.8 %reduce-scatter.5.cloned.1.call-done = bf16[64,4096]{1,0:T(8,128)(2,1)} async-done(((bf16[512,4096]{1,0:T(8,128)(2,1)}), bf16[64,4096]{1,0:T(8,128)(2,1)}) %reduce-scatter.5.cloned.1.call-update) | async-done | bytes 524304 | tf_op jit(solution)/shard_map/reduce_scatter | solution.py:60
  (4 shorter events, 0.0 us)
Async XLA Ops:
  7.2 52.0 %all-gather.9.cloned.1.call-start = ((), (), s32[]{:S(2)}) async-start(), calls=%async_computation.7 | async-start | bytes 4718592 | tf_op jit(solution)/shard_map/all_gather | solution.py:22
  7.9 80.8 %reduce-scatter.3.cloned.1.call-start = ((), (), s32[]{:S(2)}) async-start(), calls=%async_computation.2 | async-start | bytes 1572864 | tf_op jit(solution)/shard_map/reduce_scatter | solution.py:25
  69.3 112.0 %all-gather.5.cloned.1.call-start = ((), (), s32[]{:S(2)}) async-start(), calls=%async_computation.3 | async-start | bytes 8912896 | tf_op jit(solution)/shard_map/all_gather | solution.py:40
  92.5 13.6 %collective-permute-start = (bf16[512,512]{1,0:T(8,128)(2,1)S(1)}, bf16[512,512]{1,0:T(8,128)(2,1)S(1)}, u32[]{:S(2)}, u32[]{:S(2)}) collective-permute-start(bf16[512,512]{1,0:T(8,128)(2,1)S(1)} %fusion.12), channel_id=1, source_target_pairs={{0,16},{16,0},{1,17},{17,1},{2,18},{18,2},{3,19},{19,3},{4,20},{20... | collective-permute-start | bytes 1572872 | tf_op jit(solution)/shard_map/ppermute | solution.py:18
  106.0 0.8 copy-start.1
  106.8 110.9 %all-gather.7.cloned.1.call-start = ((), (), s32[]{:S(2)}) async-start(), calls=%async_computation.4 | async-start | bytes 1572864 | tf_op jit(solution)/shard_map/all_gather | solution.py:52
  108.5 88.0 %copy-start = (bf16[512,512]{1,0:T(8,128)(2,1)S(1)}, bf16[512,512]{1,0:T(8,128)(2,1)}, u32[]{:S(2)}) copy-start(bf16[512,512]{1,0:T(8,128)(2,1)} %reduce-scatter.3.cloned.1.call-done) | copy-start | bytes 1572868
  197.7 228.7 %all-reduce.2.cloned.1.call-start = ((), (), s32[]{:S(2)}) async-start(), calls=%async_computation.6 | async-start | bytes 16777216 | tf_op jit(solution)/shard_map/psum | solution.py:56
  228.2 1.2 copy-start.2
  228.2 251.2 %reduce-scatter.5.cloned.1.call-start = ((), (), s32[]{:S(2)}) async-start(), calls=%async_computation.5 | async-start | bytes 4718592 | tf_op jit(solution)/shard_map/reduce_scatter | solution.py:60
Sparse Core Ops, SparseCore 0:
  9.6 49.5 all-gather.8
  69.4 19.1 reduce-scatter.2
  107.0 74.2 all-gather.4
  197.8 19.8 all-gather.6
  228.3 198.0 all-reduce.1
  429.1 50.2 reduce-scatter.4
where the time goes:
time: 487 us; the launch traced here: 486 us
  waiting for transfers between devices  387 us (79%)
  matrix products  45.4 us (9%)
  local copies, waits for them, and re-layouts  19.5 us (4%)
  other arithmetic  18.3 us (4%)
  between operations  14.2 us (3%)
    psum x1, waiting for transfers between devices, shards(): lax.psum(local_weight.astype(jnp.bfloat16), 'view').astype(jnp.float32)  187 us
    all_gather x1, waiting for transfers between devices, shards(): piece = lax.all_gather(partner, ('row', 'col'), axis=0, tiled=True)  72.7 us
    all_gather x1, waiting for transfers between devices, shards(): hidden = lax.all_gather(inputs[0], 'col', axis=0, tiled=True)  51.2 us
    reduce_scatter x1, waiting for transfers between devices, shards(): lax.psum_scatter(lax.dot_general(columns, weight, (((0,), (1,)), ((), ())...  23.8 us
    all_gather x1, waiting for transfers between devices, shards(): grads = lax.all_gather(dpre, 'row', axis=0, tiled=True)  19.8 us
    unnamed x7, local copies, waits for them, and re-layouts  19.5 us
    reduce_scatter x1, waiting for transfers between devices, shards(): lax.psum_scatter(lax.dot_general(columns, hidden, (((0,), (1,)), ((), ())...  19.3 us
    dot_general x1, matrix products, shards(): jnp.dot(corr.astype(jnp.bfloat16), piece, preferred_element_type=jnp.floa...  15.2 us
  transfers between devices with their start and end apart: 7, of which 7 were waited for; matrix products, arithmetic and copies ran while one was open for 8% of the time, Pallas kernels for 0%

commit v1 on v0

--- a/solution.py
+++ b/solution.py
@@ -3,9 +3,39 @@
 import jax.numpy as jnp
 from jax import lax
 from jax.sharding import PartitionSpec as P
+from jax.lax import axis_index, axis_size, ppermute
 
 off_weight = 0.0051
 norm_eps = 1e-05
+
+
+def proceed_rounds_for(own_rows, in_dim):
+    f_now = list(own_rows.shape[1:])
+    f_now[in_dim] *= own_rows.shape[0]
+    t_next = jnp.moveaxis(own_rows, 0, in_dim).reshape(f_now)
+    return t_next
+
+
+def _work_heaps(original, comm_axis):
+    current_block = axis_size(comm_axis)
+    field_out = axis_index(comm_axis)
+    s_next, found_now = (current_block, field_out)
+    piece_out, b_next = (original[None], 1)
+    while b_next < s_next:
+        mat_out = tuple(((h, h ^ b_next) for h in range(s_next)))
+        even = ppermute(piece_out, axis_name=comm_axis, perm=mat_out)
+        far_arr = found_now & b_next == 0
+        g_now = jnp.where(far_arr, piece_out, even)
+        vec_out = jnp.where(far_arr, even, piece_out)
+        piece_out = jnp.concatenate([g_now, vec_out])
+        b_next *= 2
+    return piece_out
+
+
+def wait_screen(dim_at, field_in, z):
+    after = _work_heaps(z, field_in)
+    y = proceed_rounds_for(after, dim_at)
+    return y
 
 
 def from_partner(block, axis, distance):
@@ -19,7 +49,7 @@
 
 
 def shards(inputs, weight):
-    hidden = lax.all_gather(inputs[0], "col", axis=0, tiled=True)
+    hidden = wait_screen(0, "col", inputs[0])
     batch = hidden.shape[0]
     columns = weight
     pre = lax.psum_scatter(

time: 487 us -> 567 us (1.16)
  waiting for transfers between devices: 387 us -> 474 us
  local copies, waits for them, and re-layouts: 19.5 us -> 5.27 us
  starting transfers between devices: 1.96 us -> 8.44 us
  other arithmetic: 18.3 us -> 24.3 us
    ppermute x0 -> x3, waiting for transfers between devices: none -> 116 us  [_work_heaps(): even = ppermute(piece_out, axis_name=comm_axis, perm=mat_out)]
    all_gather x1 -> x0, waiting for transfers between devices: 51.2 us -> none  [shards(): hidden = lax.all_gather(inputs[0], 'col', axis=0, tiled=True)]
    reduce_scatter x1, waiting for transfers between devices: 23.8 us -> 41.1 us  [shards(): lax.psum_scatter(lax.dot_general(columns, weight, (((0,), (1,)), ((), ())...]
    unnamed x7 -> x12, local copies, waits for them, and re-layouts: 19.5 us -> 5.27 us
    ppermute x0 -> x3, starting transfers between devices: none -> 6.31 us  [_work_heaps(): even = ppermute(piece_out, axis_name=comm_axis, perm=mat_out)]
  transfers between devices with their start and end apart: 7 -> 9, of which waited for: 7 -> 9; matrix products, arithmetic and copies ran while one was open for 8% -> 4% of each run, Pallas kernels for 0% -> 0%
where the time goes in v1:
time: 567 us; the launch traced here: 566 us
  waiting for transfers between devices  474 us (84%)
  matrix products  40.5 us (7%)
  other arithmetic  24.3 us (4%)
  between operations  13.9 us (2%)
  starting transfers between devices  8.44 us (1%)
    psum x1, waiting for transfers between devices, shards(): lax.psum(local_weight.astype(jnp.bfloat16), 'view').astype(jnp.float32)  188 us
    ppermute x3, waiting for transfers between devices, _work_heaps(): even = ppermute(piece_out, axis_name=comm_axis, perm=mat_out)  116 us
    all_gather x1, waiting for transfers between devices, shards(): piece = lax.all_gather(partner, ('row', 'col'), axis=0, tiled=True)  76.2 us
    reduce_scatter x1, waiting for transfers between devices, shards(): lax.psum_scatter(lax.dot_general(columns, weight, (((0,), (1,)), ((), ())...  41.1 us
    reduce_scatter x1, waiting for transfers between devices, shards(): lax.psum_scatter(lax.dot_general(columns, hidden, (((0,), (1,)), ((), ())...  21.5 us
    all_gather x1, waiting for transfers between devices, shards(): grads = lax.all_gather(dpre, 'row', axis=0, tiled=True)  19.3 us
    dot_general x1, matrix products, shards(): jnp.dot(corr.astype(jnp.bfloat16), piece, preferred_element_type=jnp.floa...  15.1 us
    ppermute x1, waiting for transfers between devices, from_partner(): return lax.ppermute(block, axis, route)  12 us
  transfers between devices with their start and end apart: 9, of which 9 were waited for; matrix products, arithmetic and copies ran while one was open for 4% of the time, Pallas kernels for 0%

profile of v1, /device:TPU:0, one launch (start us, length us, event | category | flops | bytes accessed | tf_op | source)
XLA Modules:
  0.0 566.0 jit_solution(10785361336335381510)
XLA Ops:
  7.2 0.0 reduce-scatter.3.cloned.1.call-start
  7.2 0.6 collective-permute-start
  7.8 1.7 collective-permute-done
  9.5 1.1 broadcast_select_fusion.5
  10.6 0.1 pad_maximum_fusion.2
  10.7 3.0 collective-permute-start.1
  13.7 23.6 %collective-permute-done.1 = bf16[2,64,4096]{2,1,0:T(8,128)(2,1)} collective-permute-done((bf16[2,64,4096]{2,1,0:T(8,128)(2,1)S(1)}, bf16[2,64,4096]{2,1,0:T(8,128)(2,1)}, u32[]{:S(2)}, u32[]{:S(2)}) %collective-permute-start.1) | collective-permute-done | bytes 1048608 | tf_op jit(solution)/shard_map/ppermute | solution.py:26
  37.3 1.4 broadcast_select_fusion.3
  38.7 1.5 pad_maximum_fusion.1
  40.2 2.8 collective-permute-start.2
  42.9 0.0 slice-start
  42.9 90.5 %collective-permute-done.2 = bf16[4,64,4096]{2,1,0:T(8,128)(2,1)} collective-permute-done((bf16[4,64,4096]{2,1,0:T(8,128)(2,1)}, bf16[4,64,4096]{2,1,0:T(8,128)(2,1)}, u32[]{:S(2)}, u32[]{:S(2)}) %collective-permute-start.2) | collective-permute-done | bytes 2097184 | tf_op jit(solution)/shard_map/ppermute | solution.py:26
  133.4 1.9 broadcast_select_fusion.1
  135.3 0.0 slice-start.1
  135.3 0.4 pad_maximum_fusion
  135.7 0.0 copy-start.1
  135.7 2.1 copy-done.1
  137.8 0.0 slice-done
  137.8 1.2 slice-done.1
  139.0 5.5 fusion.2
  144.5 0.0 reduce-scatter.3.cloned.1.call-update
  144.5 0.0 all-gather.3.cloned.1.call-start
  144.5 21.5 %reduce-scatter.3.cloned.1.call-done = bf16[512,512]{0,1:T(8,128)(2,1)} async-done(((bf16[1024,512]{0,1:T(8,128)(2,1)}), bf16[512,512]{0,1:T(8,128)(2,1)}) %reduce-scatter.3.cloned.1.call-update) | async-done | bytes 524304 | tf_op jit(solution)/shard_map/reduce_scatter | solution.py:55
  166.1 1.2 convert_reduce_fusion
  167.2 1.2 fusion.6
  168.4 1.2 fusion.7
  169.6 1.5 collective-permute-start.3
  171.1 12.0 %collective-permute-done.3 = bf16[512,512]{0,1:T(8,128)(2,1)S(1)} collective-permute-done((bf16[512,512]{0,1:T(8,128)(2,1)S(1)}, bf16[512,512]{0,1:T(8,128)(2,1)S(1)}, u32[]{:S(2)}, u32[]{:S(2)}) %collective-permute-start.3) | collective-permute-done | bytes 524320 | tf_op jit(solution)/shard_map/ppermute | solution.py:48
  183.2 0.0 copy-start.2
  183.2 0.8 copy-done.2
  183.9 0.0 all-gather.3.cloned.1.call-update
  184.0 0.2 all-gather.5.cloned.1.call-start
  184.2 1.4 fusion.8
  185.6 0.0 copy-start
  185.6 76.2 %all-gather.3.cloned.1.call-done = bf16[8192,512]{0,1:T(8,128)(2,1)} async-done(((bf16[512,512]{0,1:T(8,128)(2,1)}), bf16[8192,512]{0,1:T(8,128)(2,1)}) %all-gather.3.cloned.1.call-update) | async-done | bytes 8388624 | tf_op jit(solution)/shard_map/all_gather | solution.py:70
  261.8 15.1 %fusion.14 = (f32[512]{0:T(512)S(1)}, f32[512]{0:T(512)S(1)}, f32[512,512]{0,1:T(8,128)S(1)}) fusion(bf16[512,512]{0,1:T(8,128)(2,1)S(1)} %fusion.7, bf16[512,512]{0,1:T(8,128)(2,1)} %copy-done.2, f32[512]{0:T(512)S(1)} %multiply_subtract_fusion, bf16[8192,512]{0,1:T(8,128)(2,1)} %all-gather.3.cloned.1.call-done), kind=kOutput, calls=%fused_computation.39 | convolution fusion | flops 8600420352 | bytes 10491904 | tf_op jit(solution)/shard_map/dot_general | solution.py:75
  277.0 0.0 copy-done
  277.0 1.1 fusion.12
  278.1 0.0 all-gather.5.cloned.1.call-update
  278.1 0.3 all-reduce.2.cloned.1.call-start
  278.4 19.3 %all-gather.5.cloned.1.call-done = bf16[1024,512]{0,1:T(8,128)(2,1)} async-done(((bf16[512,512]{0,1:T(8,128)(2,1)}), bf16[1024,512]{0,1:T(8,128)(2,1)}) %all-gather.5.cloned.1.call-update) | async-done | bytes 1048592 | tf_op jit(solution)/shard_map/all_gather | solution.py:82
  297.7 10.5 %convolution_convert_fusion = bf16[4096,1024]{1,0:T(8,128)(2,1)} fusion(bf16[512,4096]{1,0:T(8,128)(2,1)} %bitcast.14, bf16[1024,512]{0,1:T(8,128)(2,1)} %all-gather.5.cloned.1.call-done), kind=kOutput, calls=%fused_computation.2 | convolution fusion | flops 4299161600 | bytes 13631488 | tf_op jit(solution)/shard_map/dot_general | solution.py:83
  308.2 0.0 copy-start.3
  308.2 0.0 all-reduce.2.cloned.1.call-update
  308.2 0.0 reduce-scatter.5.cloned.1.call-start
  308.2 1.1 copy-done.3
  309.4 9.5 %convolution_convert_fusion.1 = bf16[512,4096]{1,0:T(8,128)(2,1)} fusion(bf16[1024,512]{0,1:T(8,128)(2,1)S(1)} %copy-done.3, bf16[4096,1024]{1,0:T(8,128)(2,1)} %param.3), kind=kOutput, calls=%fused_computation.3 | convolution fusion | flops 4297064448 | bytes 13631488 | tf_op jit(solution)/shard_map/dot_general | solution.py:91
  318.8 0.0 reduce-scatter.5.cloned.1.call-update
  318.9 187.5 %all-reduce.2.cloned.1.call-done = bf16[4096,1024]{1,0:T(8,128)(2,1)} async-done(((bf16[4096,1024]{1,0:T(8,128)(2,1)}), bf16[4096,1024]{1,0:T(8,128)(2,1)}) %all-reduce.2.cloned.1.call-update) | async-done | bytes 8388624 | tf_op jit(solution)/shard_map/psum | solution.py:86
  506.4 12.0 %convert_multiply_fusion = f32[4096,1024]{1,0:T(8,128)} fusion(bf16[4096,1024]{1,0:T(8,128)(2,1)} %all-reduce.2.cloned.1.call-done), kind=kLoop, calls=%fused_computation | loop fusion | flops 8388608 | bytes 25165824 | tf_op jit(solution)/shard_map/div | solution.py:86
  518.4 41.1 %reduce-scatter.5.cloned.1.call-done = bf16[64,4096]{1,0:T(8,128)(2,1)} async-done(((bf16[512,4096]{1,0:T(8,128)(2,1)}), bf16[64,4096]{1,0:T(8,128)(2,1)}) %reduce-scatter.5.cloned.1.call-update) | async-done | bytes 524304 | tf_op jit(solution)/shard_map/reduce_scatter | solution.py:90
  (5 shorter events, 0.0 us)
Async XLA Ops:
  7.2 158.9 %reduce-scatter.3.cloned.1.call-start = ((), (), s32[]{:S(2)}) async-start(), calls=%async_computation.2 | async-start | bytes 1572864 | tf_op jit(solution)/shard_map/reduce_scatter | solution.py:55
  7.2 2.3 collective-permute-start
  10.7 26.6 %collective-permute-start.1 = (bf16[2,64,4096]{2,1,0:T(8,128)(2,1)S(1)}, bf16[2,64,4096]{2,1,0:T(8,128)(2,1)}, u32[]{:S(2)}, u32[]{:S(2)}) collective-permute-start(bf16[2,64,4096]{2,1,0:T(8,128)(2,1)S(1)} %pad_maximum_fusion.2), channel_id=1, source_target_pairs={{0,2},{1,3},{2,0},{3,1},{4,6},{5,7},{6,4},{7,5},{8,10},{9,11},{10,... | collective-permute-start | bytes 3145736 | tf_op jit(solution)/shard_map/ppermute | solution.py:26
  40.2 93.3 %collective-permute-start.2 = (bf16[4,64,4096]{2,1,0:T(8,128)(2,1)}, bf16[4,64,4096]{2,1,0:T(8,128)(2,1)}, u32[]{:S(2)}, u32[]{:S(2)}) collective-permute-start(bf16[4,64,4096]{2,1,0:T(8,128)(2,1)} %pad_maximum_fusion.1), channel_id=1, source_target_pairs={{0,4},{1,5},{2,6},{3,7},{4,0},{5,1},{6,2},{7,3},{8,12},{9,13},{10,... | collective-permute-start | bytes 6291464 | tf_op jit(solution)/shard_map/ppermute | solution.py:26
  42.9 94.9 %slice-start = ((s8[8388608]{0:T(1024)(128)(4,1)}), s8[4194304]{0:T(1024)(128)(4,1)S(1)}, s32[]{:S(2)}) async-start(s8[8388608]{0:T(1024)(128)(4,1)} %bitcast.15), calls=%async_computation.7 | async-start | bytes 8388608
  135.3 3.7 slice-start.1
  135.7 2.1 copy-start.1
  144.5 117.4 %all-gather.3.cloned.1.call-start = ((), (), s32[]{:S(2)}) async-start(), calls=%async_computation.3 | async-start | bytes 8912896 | tf_op jit(solution)/shard_map/all_gather | solution.py:70
  169.6 13.5 %collective-permute-start.3 = (bf16[512,512]{0,1:T(8,128)(2,1)S(1)}, bf16[512,512]{0,1:T(8,128)(2,1)S(1)}, u32[]{:S(2)}, u32[]{:S(2)}) collective-permute-start(bf16[512,512]{0,1:T(8,128)(2,1)S(1)} %fusion.7), channel_id=1, source_target_pairs={{0,16},{16,0},{1,17},{17,1},{2,18},{18,2},{3,19},{19,3},{4,20},{20... | collective-permute-start | bytes 1572872 | tf_op jit(solution)/shard_map/ppermute | solution.py:48
  183.2 0.8 copy-start.2
  184.0 113.7 %all-gather.5.cloned.1.call-start = ((), (), s32[]{:S(2)}) async-start(), calls=%async_computation.4 | async-start | bytes 1572864 | tf_op jit(solution)/shard_map/all_gather | solution.py:82
  185.6 91.4 %copy-start = (bf16[512,512]{0,1:T(8,128)(2,1)S(1)}, bf16[512,512]{0,1:T(8,128)(2,1)}, u32[]{:S(2)}) copy-start(bf16[512,512]{0,1:T(8,128)(2,1)} %reduce-scatter.3.cloned.1.call-done) | copy-start | bytes 1572868
  278.1 228.3 %all-reduce.2.cloned.1.call-start = ((), (), s32[]{:S(2)}) async-start(), calls=%async_computation.6 | async-start | bytes 16777216 | tf_op jit(solution)/shard_map/psum | solution.py:86
  308.2 1.2 copy-start.3
  308.2 251.2 %reduce-scatter.5.cloned.1.call-start = ((), (), s32[]{:S(2)}) async-start(), calls=%async_computation.5 | async-start | bytes 4718592 | tf_op jit(solution)/shard_map/reduce_scatter | solution.py:90
Sparse Core Ops, SparseCore 0:
  144.6 21.4 reduce-scatter.2
  184.1 77.7 all-gather.2
  278.2 19.4 all-gather.4
  308.3 198.0 all-reduce.1
  509.1 50.2 reduce-scatter.4
